TPU v7x, 256 devices: a whole 4x4x8 slice. The times are simulated.
256 devices in a mesh: view: 8 (over z_hi, core), gauss: 32 (over z_lo, x, y).
Axes of the slice: x: 4, y: 4, z: 8 (z_hi: 4, z_lo: 2; z = z_hi * 2 + z_lo), core: 2. Of those that a mesh axis runs over, the one named last changes fastest.
Arguments:
- entry_grads: bfloat16 [8, 59, 655360], P('view', None, 'gauss'), may hold values from -4 to 4
- vis_ids: int32 [8, 655360], P('view', 'gauss'), may hold values from 0 to 20479
- feats: bfloat16 [256, 32, 20480], P(None, 'gauss', 'view'), may hold values from -6 to 6
- code_tab: float32 [256, 8], replicated, may hold values from -4 to 4
- subj_ids: int32 [32, 20480], P('gauss', 'view'), may hold values from 0 to 7
- bone_ids: int32 [4, 32, 20480], P(None, 'gauss', 'view'), may hold values from 0 to 23
- skin_w: float32 [4, 32, 20480], P(None, 'gauss', 'view'), may hold values from 0.05 to 0.5
- canon_pos: float32 [3, 32, 20480], P(None, 'gauss', 'view'), may hold values from -5 to 5
- bone_tf: float32 [12, 192], replicated, may hold values from -4 to 4
- w_first: bfloat16 [256, 256], replicated, may hold values from -0.375 to 0.375
- w_second: bfloat16 [256, 256], replicated, may hold values from -0.375 to 0.375
- w_third: bfloat16 [256, 256], replicated, may hold values from -0.375 to 0.375
- biases: float32 [3, 256], replicated, may hold values from -3 to 3
- w_head: bfloat16 [3, 256], replicated, may hold values from -0.375 to 0.375
Outputs:
- attr_grads: float32 [59, 32, 20480], P(None, 'gauss', 'view')
- feat_grads: bfloat16 [256, 32, 20480], P(None, 'gauss', 'view')
- skin_grads: float32 [4, 32, 20480], P(None, 'gauss', 'view')
- first_grad: float32 [256, 256], replicated
- second_grad: float32 [256, 256], replicated
- third_grad: float32 [256, 256], replicated
- bias_grads: float32 [3, 256], replicated
- head_grad: float32 [3, 256], replicated
- code_grad: float32 [256, 8], replicated
- bone_grad: float32 [12, 192], replicated
All inputs are finite; a program needn't handle non-finite values.
Results may differ from a plain program's by a relative error of at most 0.024.
Values may be sent and summed in bfloat16 or wider, within the bound.
A program may use at most 128 MiB of HBM per device.

v0:
```python
import math

import jax
import jax.numpy as jnp
from jax import lax
from jax.sharding import PartitionSpec as P

HIGH = lax.Precision.HIGHEST


def dsilu(value):
    sig = jax.nn.sigmoid(value)
    return sig * (1.0 + value * (1.0 - sig))


def over_rows(left, right):
    return lax.dot_general(
        left, right, (((1,), (1,)), ((), ())), preferred_element_type=jnp.float32
    )


def over_first(left, right):
    return lax.dot_general(
        left, right, (((0,), (0,)), ((), ())), preferred_element_type=jnp.float32
    )


def body(
    entry_grads,
    vis_ids,
    feats,
    code_tab,
    subj_ids,
    bone_ids,
    skin_w,
    canon_pos,
    bone_tf,
    w_first,
    w_second,
    w_third,
    biases,
    w_head,
):
    member_count = feats.shape[2]
    viewers = lax.axis_size("view")
    factor = 1.0 / math.sqrt(member_count * viewers * lax.axis_size("gauss"))
    partial_value = (
        jnp.zeros((entry_grads.shape[1], member_count * viewers), jnp.float32)
        .at[:, vis_ids[0]]
        .add(entry_grads[0].astype(jnp.float32))
    )
    summed = lax.psum_scatter(
        partial_value.astype(jnp.bfloat16), "view", scatter_dimension=1, tiled=True
    ).astype(jnp.float32)
    position_gradient = summed[:3]
    subjects = code_tab.shape[1]
    table_cols = bone_tf.shape[1]
    per_subject = table_cols // subjects
    subject = subj_ids[0]
    subj_hot = (subject[None, :] == jnp.arange(subjects, dtype=jnp.int32)[:, None]).astype(
        jnp.float32
    )
    code_sel = jnp.dot(code_tab, subj_hot, precision=HIGH)
    inputs = (feats[:, 0].astype(jnp.float32) + code_sel).astype(jnp.bfloat16)
    pre_one = jnp.dot(w_first, inputs, preferred_element_type=jnp.float32) + biases[0][:, None]
    act_one = jax.nn.silu(pre_one).astype(jnp.bfloat16)
    pre_two = jnp.dot(w_second, act_one, preferred_element_type=jnp.float32) + biases[1][:, None]
    act_two = jax.nn.silu(pre_two).astype(jnp.bfloat16)
    pre_three = jnp.dot(w_third, act_two, preferred_element_type=jnp.float32) + biases[2][:, None]
    act_three = jax.nn.silu(pre_three).astype(jnp.bfloat16)
    shifted_point = canon_pos[:, 0] + jnp.dot(w_head, act_three, preferred_element_type=jnp.float32)
    homogeneous_point = jnp.concatenate(
        [shifted_point, jnp.ones((1, member_count), jnp.float32)], axis=0
    )
    table_index = jnp.arange(table_cols, dtype=jnp.int32)[:, None]
    shift_acc = jnp.zeros((3, member_count), jnp.float32)
    bone_acc = jnp.zeros((12, table_cols), jnp.float32)
    skins = []
    for member_flag in range(bone_ids.shape[0]):
        column = subject * per_subject + bone_ids[member_flag, 0]
        onehot = (column[None, :] == table_index).astype(jnp.float32)
        blend_matrix = jnp.dot(bone_tf, onehot, precision=HIGH).reshape(3, 4, member_count)
        skinning_weight = skin_w[member_flag, 0]
        posed_point = jnp.sum(blend_matrix * homogeneous_point[None], axis=1)
        skins.append(jnp.sum(position_gradient * posed_point, axis=0))
        shift_acc = shift_acc + skinning_weight * jnp.sum(
            blend_matrix[:, :3] * position_gradient[:, None], axis=0
        )
        contribution = (
            (skinning_weight * position_gradient)[:, None] * homogeneous_point[None]
        ).reshape(12, member_count)
        bone_acc = bone_acc + lax.dot_general(
            contribution, onehot, (((1,), (1,)), ((), ())), precision=HIGH
        )
    shift_grad = shift_acc.astype(jnp.bfloat16)
    head = factor * over_rows(shift_grad, act_three)
    back_three = (over_first(w_head, shift_grad) * dsilu(pre_three)).astype(jnp.bfloat16)
    third = factor * over_rows(back_three, act_two)
    bias_three = factor * jnp.sum(back_three, axis=1, dtype=jnp.float32)
    bone_total = factor * bone_acc
    back_two = (over_first(w_third, back_three) * dsilu(pre_two)).astype(jnp.bfloat16)
    second = factor * over_rows(back_two, act_one)
    bias_two = factor * jnp.sum(back_two, axis=1, dtype=jnp.float32)
    back_one = (over_first(w_second, back_two) * dsilu(pre_one)).astype(jnp.bfloat16)
    first = factor * over_rows(back_one, inputs)
    bias_one = factor * jnp.sum(back_one, axis=1, dtype=jnp.float32)
    input_grad = over_first(w_first, back_one)
    code = factor * lax.dot_general(input_grad, subj_hot, (((1,), (1,)), ((), ())), precision=HIGH)
    first, second, third, bias_one, bias_two, bias_three, head, code, bone_total = lax.psum(
        (first, second, third, bias_one, bias_two, bias_three, head, code, bone_total),
        ("view", "gauss"),
    )
    bias_rows = jnp.stack([bias_one, bias_two, bias_three])
    return (
        summed[:, None, :],
        input_grad.astype(jnp.bfloat16)[:, None, :],
        jnp.stack(skins)[:, None, :],
        first,
        second,
        third,
        bias_rows,
        head,
        code,
        bone_total,
    )


def solution(mesh):
    placed = (
        P("view", None, "gauss"),
        P("view", "gauss"),
        P(None, "gauss", "view"),
        P(),
        P("gauss", "view"),
        P(None, "gauss", "view"),
        P(None, "gauss", "view"),
        P(None, "gauss", "view"),
        P(),
        P(),
        P(),
        P(),
        P(),
        P(),
    )
    return jax.shard_map(
        body,
        mesh=mesh,
        in_specs=placed,
        out_specs=(
            P(None, "gauss", "view"),
            P(None, "gauss", "view"),
            P(None, "gauss", "view"),
            P(),
            P(),
            P(),
            P(),
            P(),
            P(),
            P(),
        ),
        check_vma=False,
    )
```

profile of v0, /device:TPU:1, one launch (start us, length us, event | category | flops | bytes accessed | tf_op | source)
XLA Modules:
  0.0 489.4 jit_solution(16474853535844296468)
XLA Ops:
  8.2 4.5 convert_bitcast_fusion
  12.7 8.6 %copy.60 = f32[20480,59]{1,0:T(8,128)} copy(f32[20480,59]{0,1:T(8,128)} %convert_bitcast_fusion) | data formatting | bytes 9666560 | tf_op jit(solution)/shard_map/convert_element_type | solution.py:50
  21.3 113.8 %scatter_custom_fusion = f32[59,20480]{0,1:T(8,128)} fusion(s32[20480]{0:T(1024)S(1)} %bitcast.117, f32[20480,59]{1,0:T(8,128)} %copy.60, f32[]{:T(128)} %constant.6.clone.1), kind=kCustom, calls=%fused_computation.2 | custom fusion | flops 1208320 | bytes 4833792 | tf_op jit(solution)/shard_map/scatter-add | solution.py:50
  135.1 8.3 %copy.61 = bf16[59,20480]{1,0:T(8,128)(2,1)} copy(f32[59,20480]{0,1:T(8,128)} %scatter_custom_fusion) | data formatting | bytes 7249920 | tf_op jit(solution)/shard_map/scatter-add | solution.py:50
  143.5 1.2 copy-done.4
  149.3 1.3 fusion.9
  150.6 2.3 multiply_convert_fusion.2
  153.0 2.3 multiply_convert_fusion.1
  155.3 2.4 multiply_convert_fusion
  157.7 1.1 copy-done.3
  159.7 31.7 %reduce-scatter.2.cloned.1.call-done = bf16[59,2560]{1,0:T(8,128)(2,1)} async-done(((bf16[59,20480]{1,0:T(8,128)(2,1)}), bf16[59,2560]{1,0:T(8,128)(2,1)}) %reduce-scatter.2.cloned.1.call-update) | async-done | bytes 302096 | tf_op jit(solution)/shard_map/reduce_scatter | solution.py:52
  192.5 1.1 fusion.40
  193.6 1.3 broadcast_multiply_fusion.7
  194.9 1.8 convert_reduce_fusion
  196.7 1.7 convert_reduce_fusion.1
  198.4 1.7 convert_reduce_fusion.2
  201.4 1.5 convolution_multiply_fusion.2
  202.9 1.3 convolution_multiply_fusion.1
  204.2 1.3 convolution_multiply_fusion
  205.4 2.2 convolution_multiply_fusion.4
  207.6 1.4 copy.63
  209.1 1.2 convert_bitcast_fusion.1
  210.3 2.4 copy.64
  213.7 1.7 fusion.14
  215.5 1.7 fusion.15
  217.2 1.7 fusion.16
  219.0 1.7 fusion.21
  221.7 81.0 %all-reduce.1 = (f32[1,256]{1,0:T(1,128)S(1)}, f32[1,256]{1,0:T(1,128)S(1)}, f32[1,256]{1,0:T(1,128)S(1)}, f32[3,256]{1,0:T(4,128)}, f32[256,8]{0,1:T(8,128)}, /*index=5*/f32[12,192]{1,0:T(8,128)}) all-reduce(f32[1,256]{1,0:T(1,128)S(1)} %bitcast.118, ...), channel_id=1, replica_groups=mesh['view'=8,'gauss'=32] {'view','gauss'}, use_global_device_ids=true, to_apply=%region_22.23 | all-reduce | flops 5888 | bytes 47104 | tf_op jit(solution)/shard_map/psum | solution.py:109
  303.3 174.2 %all-reduce.5.cloned.1.call-done = (f32[256,256]{1,0:T(8,128)}, f32[256,256]{1,0:T(8,128)}, f32[256,256]{1,0:T(8,128)}) async-done(((f32[256,256]{1,0:T(8,128)}, f32[256,256]{1,0:T(8,128)}, f32[256,256]{1,0:T(8,128)}), (f32[256,256]{1,0:T(8,128)}, f32[256,256]{1,0:T(8,128)}, f32[256,256]{1,0:T(8,128)})) %all-reduce.5.cloned.1.call-update) | async-done | bytes 786448 | tf_op jit(solution)/shard_map/psum | solution.py:109
  477.5 1.7 copy.70
  479.2 1.7 copy.71
  480.9 1.7 copy.72
  (111 shorter events, 11.7 us)
Async XLA Ops:
  7.2 148.1 %copy-start = (bf16[256,256]{1,0:T(8,128)(2,1)S(1)}, bf16[256,256]{1,0:T(8,128)(2,1)}, u32[]{:S(2)}) copy-start(bf16[256,256]{1,0:T(8,128)(2,1)} %param.25) | copy-start | bytes 393220
  7.2 184.2 %reduce-scatter.2.cloned.1.call-start = ((), (), s32[]{:S(2)}) async-start(), calls=%async_computation.1 | async-start | bytes 2949120 | tf_op jit(solution)/shard_map/reduce_scatter | solution.py:52
  143.4 2.1 copy-start.18
  143.4 2.1 copy-start.25
  143.4 2.9 copy-start.33
  143.4 5.9 %copy-start.27 = (f32[3,256]{1,0:T(4,128)S(1)}, f32[3,256]{1,0:T(4,128)}, u32[]{:S(2)}) copy-start(f32[3,256]{1,0:T(4,128)} %param.26) | copy-start | bytes 9220
  143.4 5.9 %copy-start.26 = (f32[256,8]{0,1:T(8,128)S(1)}, f32[256,8]{0,1:T(8,128)}, u32[]{:S(2)}) copy-start(f32[256,8]{0,1:T(8,128)} %param.17) | copy-start | bytes 24580
  143.4 334.1 %all-reduce.5.cloned.1.call-start = ((), (), s32[]{:S(2)}) async-start(), calls=%async_computation.2 | async-start | bytes 1572864 | tf_op jit(solution)/shard_map/psum | solution.py:109
  145.6 2.1 copy-start.22
  145.6 2.9 copy-start.23
  145.7 4.9 %copy-start.24 = (s32[2560]{0:T(1024)}, s32[2560]{0:T(1024)S(1)}, u32[]{:S(2)}) copy-start(s32[2560]{0:T(1024)S(1)} %get-tuple-element.56) | copy-start | bytes 30724
  146.9 3.7 copy-start.11
  150.6 2.3 copy-start.1
  150.6 2.3 copy-start.32
  153.0 2.3 copy-start.5
  155.3 2.4 copy-start.7
  155.3 3.5 copy-start.14
  155.3 3.5 copy-start.28
  155.3 3.9 copy-start.19
  191.4 3.5 copy-start.36
  194.9 1.8 copy-start.13
  200.1 2.8 copy-start.6
  201.4 2.8 copy-start.8
  209.1 3.7 copy-start.17
  209.1 3.7 copy-start.16
  209.1 3.7 copy-start.15
  209.1 4.4 copy-start.29
  209.1 4.4 copy-start.30
  209.1 4.4 copy-start.31
  209.1 4.5 copy-start.9
  209.1 4.5 copy-start.10
  217.2 4.5 copy-start.20
  (7 other events, 9.5 us)
Sparse Core Ops, SparseCore 0:
  143.5 47.8 reduce-scatter.1
  219.1 258.3 all-reduce.4
where the time goes:
time: 491 us; the launch traced here: 489 us
  waiting for transfers between devices  206 us (42%)
  other arithmetic  124 us (25%)
  blocking collectives  81 us (16%)
  local copies, waits for them, and re-layouts  32.5 us (7%)
  matrix products  31.1 us (6%)
  between operations  14.5 us (3%)
    psum x1, waiting for transfers between devices, body(): lax.psum((first, second, third, bias_one, bias_two, bias_three, head, cod...  174 us
    scatter-add x1, other arithmetic, body(): partial_value = jnp.zeros((entry_grads.shape[1], member_count * viewers),...  114 us
    psum x1, blocking collectives, body(): lax.psum((first, second, third, bias_one, bias_two, bias_three, head, cod...  81 us
    reduce_scatter x1, waiting for transfers between devices, body(): lax.psum_scatter(partial_value.astype(jnp.bfloat16), 'view', scatter_dime...  31.7 us
    unnamed x80, local copies, waits for them, and re-layouts  13.5 us
  transfers between devices with their start and end apart: 2, of which 2 were waited for; matrix products, arithmetic and copies ran while one was open for 3% of the time, Pallas kernels for 0%

commit v1 on v0

--- a/solution.py
+++ b/solution.py
@@ -1,8 +1,11 @@
+import functools
 import math
 
 import jax
 import jax.numpy as jnp
 from jax import lax
+from jax.experimental import pallas as pl
+from jax.experimental.pallas import tpu as pltpu
 from jax.sharding import PartitionSpec as P
 
 HIGH = lax.Precision.HIGHEST
@@ -23,6 +26,191 @@
     return lax.dot_general(
         left, right, (((0,), (0,)), ((), ())), preferred_element_type=jnp.float32
     )
+
+
+ENTRY_COUNT, ATTRS, GAUSS = 20480, 59, 20480
+HALF = GAUSS // 2
+BLOCK = 128
+def scatter_kernel(K, UF, rows_ref, ids_ref, grads_ref, out_ref, vals_a, vals_b, *accs):
+    def zero(i, c):
+        for a in accs:
+            a[pl.ds(pl.multiple_of(i * 128, 128), 128), :] = jnp.zeros((128, 128), jnp.float32)
+        return c
+    lax.fori_loop(0, HALF // 128, zero, 0)
+    def tr(off, vals):
+        for b in range(BLOCK // 128):
+            o = pl.multiple_of(off + b * 128, 128)
+            x = grads_ref[0, :, pl.ds(o, 128)].astype(jnp.float32)
+            x = jnp.concatenate([x, jnp.zeros((64 - ATTRS, 128), jnp.float32)], axis=0)
+            hi = ids_ref[:, pl.ds(o, 128)] >= HALF
+            m = jnp.concatenate([jnp.where(hi, 0.0, x), jnp.where(hi, x, 0.0)], axis=0)
+            vals[b * 128:(b + 1) * 128, :] = m.T
+    def rmw(off, vals):
+        for j in range(BLOCK // K):
+            r = [rows_ref[off + j * K + k] for k in range(K)]
+            new = [accs[k][pl.ds(r[k], 1), :] + vals[j * K + k:j * K + k + 1, :] for k in range(K)]
+            for k in range(K):
+                accs[k][pl.ds(r[k], 1), :] = new[k]
+    tr(0, vals_a)
+    def step(i, c):
+        off = pl.multiple_of(i * (2 * BLOCK), 2 * BLOCK)
+        tr(off + BLOCK, vals_b)
+        rmw(off, vals_a)
+        tr(jnp.minimum(off + 2 * BLOCK, ENTRY_COUNT - BLOCK), vals_a)
+        rmw(off + BLOCK, vals_b)
+        return c
+    lax.fori_loop(0, ENTRY_COUNT // (2 * BLOCK), step, 0)
+    def fin(i, c):
+        for u in range(UF):
+            off = pl.multiple_of(i * (128 * UF) + u * 128, 128)
+            s = accs[0][pl.ds(off, 128), :]
+            for a in accs[1:]:
+                s = s + a[pl.ds(off, 128), :]
+            t = s.T.astype(jnp.bfloat16)
+            out_ref[:, pl.ds(off, 128)] = t[:ATTRS]
+            out_ref[:, pl.ds(pl.multiple_of(HALF + off, 128), 128)] = t[64:64 + ATTRS]
+        return c
+    lax.fori_loop(0, HALF // (128 * UF), fin, 0)
+
+def scatter(grads, ids, K=8, UF=4):
+    ids1 = ids.reshape(-1)
+    rows = jnp.where(ids1 >= HALF, ids1 - HALF, ids1)
+    return pl.pallas_call(
+        functools.partial(scatter_kernel, K, UF),
+        out_shape=jax.ShapeDtypeStruct((ATTRS, GAUSS), jnp.bfloat16),
+        in_specs=[pl.BlockSpec(memory_space=pltpu.SMEM), pl.BlockSpec(memory_space=pltpu.VMEM), pl.BlockSpec(memory_space=pltpu.VMEM)],
+        out_specs=pl.BlockSpec(memory_space=pltpu.VMEM),
+        scratch_shapes=[pltpu.VMEM((BLOCK, 128), jnp.float32)] * 2 + [pltpu.VMEM((HALF, 128), jnp.float32)] * K,
+        compiler_params=pltpu.CompilerParams(vmem_limit_bytes=62 * 1024 * 1024),
+    )(rows, ids.reshape(1, -1), grads)
+
+
+MESH = pl.DeviceIdType.MESH
+PIECE, PLANE, DEPTH = 56, 16, 8
+
+
+def place():
+    view, gauss = lax.axis_index("view"), lax.axis_index("gauss")
+    return view // 2, lax.rem(view, 2), gauss // PLANE, lax.rem(gauss, PLANE)
+
+
+def plane_peer(step):
+    high, core, low, spot = place()
+    return (high * 2 + core, low * PLANE + lax.rem(spot + step, PLANE))
+
+
+def depth_peer(step):
+    high, core, low, spot = place()
+    level = lax.rem(high * 2 + low + step, DEPTH)
+    return ((level // 2) * 2 + core, lax.rem(level, 2) * PLANE + spot)
+
+
+def core_peer():
+    high, core, low, spot = place()
+    return (high * 2 + 1 - core, low * PLANE + spot)
+
+
+def greet(barrier, peers, count):
+    def one(step, carry):
+        pl.semaphore_signal(barrier, inc=1, device_id=peers(step), device_id_type=MESH)
+        return carry
+
+    lax.fori_loop(1, count, one, 0)
+
+
+def remote(src, dst, sems, step, peer):
+    return pltpu.make_async_remote_copy(
+        src_ref=src,
+        dst_ref=dst,
+        send_sem=sems.at[0, step],
+        recv_sem=sems.at[1, step],
+        device_id=peer,
+        device_id_type=MESH,
+    )
+
+
+def each(count, action):
+    def one(step, carry):
+        action(step)
+        return carry
+
+    lax.fori_loop(1, count, one, 0)
+
+
+def reduce_all(pay, out, near, plane, depth, sems_near, sems_plane, sems_depth, sems_back):
+    high, core, low, spot = place()
+    level = high * 2 + low
+    swap = remote(pay.at[1 - core], near, sems_near, 0, core_peer())
+    swap.start()
+    swap.wait()
+    near[...] = near[...] + pay[core]
+
+    def plane_copy(step):
+        return remote(near.at[lax.rem(spot + step, PLANE)], plane.at[spot], sems_plane, step, plane_peer(step))
+
+    each(PLANE, lambda step: plane_copy(step).start())
+    plane[spot] = near[spot]
+    each(PLANE, lambda step: plane_copy(step).wait())
+    total = plane[0]
+    for index in range(1, PLANE):
+        total = total + plane[index]
+    depth[level] = total
+
+    def depth_copy(step):
+        return remote(depth.at[level], depth.at[level], sems_depth, step, depth_peer(step))
+
+    each(DEPTH, lambda step: depth_copy(step).start())
+    each(DEPTH, lambda step: depth_copy(step).wait())
+    total = depth[0]
+    for index in range(1, DEPTH):
+        total = total + depth[index]
+    out[core, spot] = total
+
+    def back_copy(step):
+        return remote(out.at[core, spot], out.at[core, spot], sems_back, step, plane_peer(step))
+
+    each(PLANE, lambda step: back_copy(step).start())
+    each(PLANE, lambda step: back_copy(step).wait())
+    last = remote(out.at[core], out.at[core], sems_near, 1, core_peer())
+    last.start()
+    last.wait()
+
+
+def reduce_kernel(pay, out, near, plane, depth, sems_near, sems_plane, sems_depth, sems_back):
+    barrier = pltpu.get_barrier_semaphore()
+    greet(barrier, plane_peer, PLANE)
+    greet(barrier, depth_peer, DEPTH)
+    pl.semaphore_signal(barrier, inc=1, device_id=core_peer(), device_id_type=MESH)
+    pl.semaphore_wait(barrier, PLANE - 1 + DEPTH - 1 + 1)
+    reduce_all(pay, out, near, plane, depth, sems_near, sems_plane, sems_depth, sems_back)
+
+
+REDUCE_SCRATCH = [
+    pltpu.VMEM((PLANE, PIECE, 128), jnp.float32),
+    pltpu.VMEM((PLANE, PIECE, 128), jnp.float32),
+    pltpu.VMEM((DEPTH, PIECE, 128), jnp.float32),
+    pltpu.SemaphoreType.DMA((2, 2)),
+    pltpu.SemaphoreType.DMA((2, PLANE)),
+    pltpu.SemaphoreType.DMA((2, DEPTH)),
+    pltpu.SemaphoreType.DMA((2, PLANE)),
+]
+
+
+def reduce_call(pay):
+    return pl.pallas_call(
+        reduce_kernel,
+        out_shape=jax.ShapeDtypeStruct((2, PLANE, PIECE, 128), jnp.float32),
+        in_specs=[pl.BlockSpec(memory_space=pltpu.VMEM)],
+        out_specs=pl.BlockSpec(memory_space=pltpu.VMEM),
+        scratch_shapes=REDUCE_SCRATCH,
+        compiler_params=pltpu.CompilerParams(collective_id=0, has_side_effects=True),
+        name="reduce_all",
+    )(pay)
+
+
+def pack(first, second, third, small):
+    rows = jnp.concatenate([first, second, third, small], axis=0)
+    return jnp.stack([rows[:, :128], rows[:, 128:]]).reshape(2, PLANE, PIECE, 128)
 
 
 def body(
@@ -44,14 +232,10 @@
     member_count = feats.shape[2]
     viewers = lax.axis_size("view")
     factor = 1.0 / math.sqrt(member_count * viewers * lax.axis_size("gauss"))
-    partial_value = (
-        jnp.zeros((entry_grads.shape[1], member_count * viewers), jnp.float32)
-        .at[:, vis_ids[0]]
-        .add(entry_grads[0].astype(jnp.float32))
-    )
-    summed = lax.psum_scatter(
-        partial_value.astype(jnp.bfloat16), "view", scatter_dimension=1, tiled=True
-    ).astype(jnp.float32)
+    partial_value = scatter(entry_grads, vis_ids)
+    summed = lax.psum_scatter(partial_value, "view", scatter_dimension=1, tiled=True).astype(
+        jnp.float32
+    )
     position_gradient = summed[:3]
     subjects = code_tab.shape[1]
     table_cols = bone_tf.shape[1]
@@ -93,24 +277,35 @@
             contribution, onehot, (((1,), (1,)), ((), ())), precision=HIGH
         )
     shift_grad = shift_acc.astype(jnp.bfloat16)
-    head = factor * over_rows(shift_grad, act_three)
+    head = over_rows(shift_grad, act_three)
     back_three = (over_first(w_head, shift_grad) * dsilu(pre_three)).astype(jnp.bfloat16)
-    third = factor * over_rows(back_three, act_two)
-    bias_three = factor * jnp.sum(back_three, axis=1, dtype=jnp.float32)
-    bone_total = factor * bone_acc
+    third = over_rows(back_three, act_two)
+    bias_three = jnp.sum(back_three, axis=1, dtype=jnp.float32)
+    bone_total = bone_acc
     back_two = (over_first(w_third, back_three) * dsilu(pre_two)).astype(jnp.bfloat16)
-    second = factor * over_rows(back_two, act_one)
-    bias_two = factor * jnp.sum(back_two, axis=1, dtype=jnp.float32)
+    second = over_rows(back_two, act_one)
+    bias_two = jnp.sum(back_two, axis=1, dtype=jnp.float32)
     back_one = (over_first(w_second, back_two) * dsilu(pre_one)).astype(jnp.bfloat16)
-    first = factor * over_rows(back_one, inputs)
-    bias_one = factor * jnp.sum(back_one, axis=1, dtype=jnp.float32)
+    first = over_rows(back_one, inputs)
+    bias_one = jnp.sum(back_one, axis=1, dtype=jnp.float32)
     input_grad = over_first(w_first, back_one)
-    code = factor * lax.dot_general(input_grad, subj_hot, (((1,), (1,)), ((), ())), precision=HIGH)
-    first, second, third, bias_one, bias_two, bias_three, head, code, bone_total = lax.psum(
-        (first, second, third, bias_one, bias_two, bias_three, head, code, bone_total),
-        ("view", "gauss"),
-    )
-    bias_rows = jnp.stack([bias_one, bias_two, bias_three])
+    code = lax.dot_general(subj_hot, input_grad, (((1,), (1,)), ((), ())), precision=HIGH)
+    small = jnp.concatenate(
+        [
+            head,
+            bias_one[None],
+            bias_two[None],
+            bias_three[None],
+            code,
+            jnp.pad(bone_total, ((0, 128 - 26), (0, 256 - table_cols))),
+        ],
+        axis=0,
+    )
+    whole = factor * reduce_call(pack(first, second, third, small)).reshape(2, 896, 128)
+    whole = jnp.concatenate([whole[0], whole[1]], axis=1)
+    first, second, third = whole[:256], whole[256:512], whole[512:768]
+    head, bias_rows, code = whole[768:771], whole[771:774], whole[774:782].T
+    bone_total = whole[782:794, :table_cols]
     return (
         summed[:, None, :],
         input_grad.astype(jnp.bfloat16)[:, None, :],

time: 491 us -> 166 us (0.34)
  waiting for transfers between devices: 206 us -> 32.2 us
  other arithmetic: 124 us -> 10.8 us
  blocking collectives: 81 us -> 0 us
  Pallas kernels: 0 us -> 66.4 us
  local copies, waits for them, and re-layouts: 32.5 us -> 14.4 us
    psum x1 -> x0, waiting for transfers between devices: 174 us -> none  [body(): lax.psum((first, second, third, bias_one, bias_two, bias_three, head, cod...]
    scatter-add x1 -> x0, other arithmetic: 114 us -> none  [body(): partial_value = jnp.zeros((entry_grads.shape[1], member_count * viewers),...]
    psum x1 -> x0, blocking collectives: 81 us -> none  [body(): lax.psum((first, second, third, bias_one, bias_two, bias_three, head, cod...]
    pallas_call x0 -> x2, Pallas kernels: none -> 66.4 us  [the longest x1 39.1 us: reduce_call(): pl.pallas_call(reduce_kernel, out_shape=jax.ShapeDtypeStruct((2, PLANE, P...]
    convert_element_type x1 -> x0, local copies, waits for them, and re-layouts: 8.61 us -> none  [body(): entry_grads[0].astype(jnp.float32)]
    scatter-add x1 -> x0, local copies, waits for them, and re-layouts: 8.29 us -> none  [body(): partial_value = jnp.zeros((entry_grads.shape[1], member_count * viewers),...]
    unnamed x80 -> x71, local copies, waits for them, and re-layouts: 13.5 us -> 7.44 us
  transfers between devices with their start and end apart: 2 -> 1, of which waited for: 2 -> 1; matrix products, arithmetic and copies ran while one was open for 3% -> 9% of each run, Pallas kernels for 0% -> 0%
where the time goes in v1:
time: 166 us
  Pallas kernels  66.4 us (40%)
  waiting for transfers between devices  32.2 us (19%)
  matrix products  27.6 us (17%)
  between operations  14.5 us (9%)
  local copies, waits for them, and re-layouts  14.4 us (9%)
  other arithmetic  10.8 us (7%)
    pallas_call x1, Pallas kernels, reduce_call(): pl.pallas_call(reduce_kernel, out_shape=jax.ShapeDtypeStruct((2, PLANE, P...  39.1 us
    reduce_scatter x1, waiting for transfers between devices, body(): lax.psum_scatter(partial_value, 'view', scatter_dimension=1, tiled=True)  32.2 us
    pallas_call x1, Pallas kernels, scatter(): pl.pallas_call(functools.partial(scatter_kernel, K, UF), out_shape=jax.Sh...  27.3 us
    unnamed x71, local copies, waits for them, and re-layouts  7.44 us
    dot_general x4, matrix products, over_first(): lax.dot_general(left, right, (((0,), (0,)), ((), ())), preferred_element_...  6.43 us
    dot_general x4, matrix products, body(): lax.dot_general(contribution, onehot, (((1,), (1,)), ((), ())), precision...  4.13 us
    dot_general x4, matrix products, over_rows(): lax.dot_general(left, right, (((1,), (1,)), ((), ())), preferred_element_...  3.9 us
    concatenate x1, local copies, waits for them, and re-layouts, pack(): rows = jnp.concatenate([first, second, third, small], axis=0)  3.51 us
  transfers between devices with their start and end apart: 1, of which 1 were waited for; matrix products, arithmetic and copies ran while one was open for 9% of the time, Pallas kernels for 0%

profile of v1, /device:TPU:1, one launch (start us, length us, event | category | flops | bytes accessed | tf_op | source)
XLA Modules:
  0.0 165.9 jit_solution(7114355144330803558)
XLA Ops:
  7.2 1.6 compare_select_fusion.rows_ref
  8.8 27.3 %shard_map.213 = bf16[59,20480]{1,0:T(8,128)(2,1)} custom-call(s32[20480]{0:T(1024)} %compare_select_fusion.rows_ref, s32[1,20480]{1,0:T(1,128)} %ids_ref.1, bf16[1,59,20480]{2,1,0:T(8,128)(2,1)} %grads_ref.1), custom_call_target="tpu_custom_call" | custom-call | tf_op jit(solution)/shard_map/pallas_call | solution.py:78
  36.1 0.7 copy-done.13
  40.7 0.8 copy.24
  41.5 1.3 fusion.7
  42.8 2.3 %multiply_convert_fusion.2 = (bf16[256,2560]{0,1:T(8,128)(2,1)S(1)}, f32[256,2560]{0,1:T(8,128)}) fusion(f32[256]{0:T(256)S(1)} %bitcast.132, bf16[256,2560]{0,1:T(8,128)(2,1)S(1)} %fusion.7, bf16[256,256]{1,0:T(8,128)(2,1)S(1)} %copy-done.7), kind=kOutput, calls=%fused_computation.31 | convolution fusion | flops 339476480 | bytes 5374976 | tf_op jit(solution)/shard_map/dot_general | solution.py:249
  45.1 2.3 %multiply_convert_fusion.1 = (bf16[256,2560]{0,1:T(8,128)(2,1)S(1)}, f32[256,2560]{0,1:T(8,128)}) fusion(f32[256]{0:T(256)S(1)} %bitcast.131, bf16[256,2560]{0,1:T(8,128)(2,1)S(1)} %get-tuple-element.68, bf16[256,256]{1,0:T(8,128)(2,1)S(1)} %copy-done.28), kind=kOutput, calls=%fused_computation.29 | convolution fusion | flops 339476480 | bytes 5374976 | tf_op jit(solution)/shard_map/dot_general | solution.py:251
  47.5 2.4 %multiply_convert_fusion = (bf16[256,2560]{0,1:T(8,128)(2,1)S(1)}, f32[256,2560]{0,1:T(8,128)}) fusion(f32[256]{0:T(256)S(1)} %bitcast.130, bf16[256,2560]{0,1:T(8,128)(2,1)S(1)} %get-tuple-element.70, bf16[256,256]{1,0:T(8,128)(2,1)S(1)} %copy-done), kind=kOutput, calls=%fused_computation.27 | convolution fusion | flops 339476480 | bytes 5374976 | tf_op jit(solution)/shard_map/dot_general | solution.py:253
  51.0 1.0 multiply_reduce_fusion.3
  52.0 32.2 %reduce-scatter.2.cloned.1.call-done = bf16[59,2560]{1,0:T(8,128)(2,1)} async-done(((bf16[59,20480]{1,0:T(8,128)(2,1)}), bf16[59,2560]{1,0:T(8,128)(2,1)}) %reduce-scatter.2.cloned.1.call-update) | async-done | bytes 302096 | tf_op jit(solution)/shard_map/reduce_scatter | solution.py:236
  84.2 0.9 slice.111
  85.3 1.1 fusion.47
  86.4 1.6 broadcast_multiply_fusion.8
  88.0 0.9 fusion.53
  88.9 2.5 %convert_reduce_fusion = (f32[256]{0:T(256)}, bf16[256,2560]{0,1:T(8,128)(2,1)S(1)}) fusion(f32[256,2560]{0,1:T(8,128)S(1)} %copy-done.33, bf16[3,2560]{1,0:T(4,128)(2,1)S(1)} %get-tuple-element.60, bf16[3,256]{1,0:T(4,128)(2,1)} %param.27), kind=kOutput, calls=%fused_computation.24 | convolution fusion | flops 11140864 | bytes 3950080 | tf_op jit(solution)/shard_map/dot_general | solution.py:26
  91.4 1.2 fusion.52
  93.3 1.7 %convert_reduce_fusion.1 = (f32[256]{0:T(256)}, bf16[256,2560]{0,1:T(8,128)(2,1)S(1)}) fusion(f32[256,2560]{0,1:T(8,128)S(1)} %copy-done.32, bf16[256,2560]{0,1:T(8,128)(2,1)S(1)} %get-tuple-element.79, bf16[256,256]{1,0:T(8,128)(2,1)S(1)} %copy-done), kind=kOutput, calls=%fused_computation.25 | convolution fusion | flops 342753024 | bytes 5374976 | tf_op jit(solution)/shard_map/dot_general | solution.py:26
  95.9 0.9 copy-done.31
  96.8 1.7 %convert_reduce_fusion.2 = (f32[256]{0:T(256)}, bf16[256,2560]{0,1:T(8,128)(2,1)S(1)}) fusion(f32[256,2560]{0,1:T(8,128)S(1)} %copy-done.31, bf16[256,2560]{0,1:T(8,128)(2,1)S(1)} %get-tuple-element.77, bf16[256,256]{1,0:T(8,128)(2,1)S(1)} %copy-done.29), kind=kOutput, calls=%fused_computation.26 | convolution fusion | flops 342753024 | bytes 5374976 | tf_op jit(solution)/shard_map/dot_general | solution.py:26
  98.5 1.2 fusion.50
  100.2 1.6 fusion.34
  102.5 1.2 fusion.14
  103.8 1.0 fusion.13
  104.8 1.0 fusion.12
  105.8 1.0 fusion.18
  107.5 3.5 %concatenate.11 = f32[896,256]{1,0:T(8,128)S(1)} concatenate(f32[256,256]{1,0:T(8,128)} %fusion.50, f32[256,256]{1,0:T(8,128)S(1)} %fusion.51, f32[256,256]{1,0:T(8,128)S(1)} %copy-done.6, f32[3,256]{1,0:T(4,128)S(1)} %copy-done.15, f32[1,256]{1,0:T(1,128)} %bitcast.129, f32[1,256]{1,0:T(1,128)} %bitcast.128, f32[1,256]{1,0:T(1,128)} %bitcast.127, f32[8,256]{1,0:T(8,128)} %fusion.34, ...), dimensions={0} | concatenate | bytes 1835008 | tf_op jit(solution)/shard_map/concatenate | solution.py:212
  111.1 1.0 pad_maximum_fusion.pay
  112.1 39.1 %reduce_all.1 = f32[2,16,56,128]{3,2,1,0:T(8,128)} custom-call(f32[2,16,56,128]{3,2,1,0:T(8,128)} %pad_maximum_fusion.pay), custom_call_target="tpu_custom_call" | custom-call | tf_op jit(solution)/shard_map/reduce_all/pallas_call | solution.py:200
  151.2 1.3 broadcast_multiply_fusion
  154.3 0.9 fusion.29
  155.2 1.4 copy.25
  157.5 1.6 copy.26
  (102 shorter events, 11.3 us)
Async XLA Ops:
  7.2 40.3 %copy-start = (bf16[256,256]{1,0:T(8,128)(2,1)S(1)}, bf16[256,256]{1,0:T(8,128)(2,1)}, u32[]{:S(2)}) copy-start(bf16[256,256]{1,0:T(8,128)(2,1)} %param.25) | copy-start | bytes 393220
  7.2 77.0 %reduce-scatter.2.cloned.1.call-start = ((), (), s32[]{:S(2)}) async-start(), calls=%async_computation.1 | async-start | bytes 2949120 | tf_op jit(solution)/shard_map/reduce_scatter | solution.py:236
  36.1 0.8 copy-start.24
  36.1 1.5 copy-start.30
  36.1 4.6 %copy-start.1 = (bf16[256,1,2560]{2,0,1:T(8,128)(2,1)S(1)}, bf16[256,1,2560]{2,0,1:T(8,128)(2,1)}, u32[]{:S(2)}) copy-start(bf16[256,1,2560]{2,0,1:T(8,128)(2,1)} %param.16) | copy-start | bytes 3932164
  37.0 2.9 %copy-start.18 = (s32[2560]{0:T(1024)}, s32[2560]{0:T(1024)S(1)}, u32[]{:S(2)}) copy-start(s32[2560]{0:T(1024)S(1)} %get-tuple-element.26) | copy-start | bytes 30724
  37.0 2.9 %copy-start.22 = (s32[2560]{0:T(1024)}, s32[2560]{0:T(1024)S(1)}, u32[]{:S(2)}) copy-start(s32[2560]{0:T(1024)S(1)} %get-tuple-element.25) | copy-start | bytes 30724
  37.0 3.6 %copy-start.20 = (s32[2560]{0:T(1024)}, s32[2560]{0:T(1024)S(1)}, u32[]{:S(2)}) copy-start(s32[2560]{0:T(1024)S(1)} %get-tuple-element.27) | copy-start | bytes 30724
  38.3 3.2 %copy-start.26 = (f32[3,256]{1,0:T(4,128)S(1)}, f32[3,256]{1,0:T(4,128)}, u32[]{:S(2)}) copy-start(f32[3,256]{1,0:T(4,128)} %param.26) | copy-start | bytes 9220
  38.3 3.2 %copy-start.25 = (f32[256,8]{0,1:T(8,128)S(1)}, f32[256,8]{0,1:T(8,128)}, u32[]{:S(2)}) copy-start(f32[256,8]{0,1:T(8,128)} %param.17) | copy-start | bytes 24580
  40.7 2.1 %copy-start.7 = (bf16[256,256]{1,0:T(8,128)(2,1)S(1)}, bf16[256,256]{1,0:T(8,128)(2,1)}, u32[]{:S(2)}) copy-start(bf16[256,256]{1,0:T(8,128)(2,1)} %param.23) | copy-start | bytes 393220
  42.8 2.3 %copy-start.28 = (bf16[256,256]{1,0:T(8,128)(2,1)S(1)}, bf16[256,256]{1,0:T(8,128)(2,1)}, u32[]{:S(2)}) copy-start(bf16[256,256]{1,0:T(8,128)(2,1)} %param.24) | copy-start | bytes 393220
  45.1 2.3 %copy-start.2 = (bf16[256,2560]{0,1:T(8,128)(2,1)}, bf16[256,2560]{0,1:T(8,128)(2,1)S(1)}, u32[]{:S(2)}) copy-start(bf16[256,2560]{0,1:T(8,128)(2,1)S(1)} %get-tuple-element.68) | copy-start | bytes 3932164
  47.4 2.4 %copy-start.4 = (bf16[256,2560]{0,1:T(8,128)(2,1)}, bf16[256,2560]{0,1:T(8,128)(2,1)S(1)}, u32[]{:S(2)}) copy-start(bf16[256,2560]{0,1:T(8,128)(2,1)S(1)} %get-tuple-element.70) | copy-start | bytes 3932164
  47.5 2.4 %copy-start.9 = (f32[3,1,2560]{2,1,0:T(1,128)S(1)}, f32[3,1,2560]{2,1,0:T(1,128)}, u32[]{:S(2)}) copy-start(f32[3,1,2560]{2,1,0:T(1,128)} %param.21) | copy-start | bytes 92164
  47.5 2.4 %copy-start.27 = (bf16[3,256]{1,0:T(4,128)(2,1)S(1)}, bf16[3,256]{1,0:T(4,128)(2,1)}, u32[]{:S(2)}) copy-start(bf16[3,256]{1,0:T(4,128)(2,1)} %param.27) | copy-start | bytes 4612
  47.5 2.9 %copy-start.14 = (f32[4,1,2560]{2,1,0:T(1,128)S(1)}, f32[4,1,2560]{2,1,0:T(1,128)}, u32[]{:S(2)}) copy-start(f32[4,1,2560]{2,1,0:T(1,128)} %param.20) | copy-start | bytes 122884
  84.2 4.7 %copy-start.33 = (f32[256,2560]{0,1:T(8,128)S(1)}, f32[256,2560]{0,1:T(8,128)}, u32[]{:S(2)}) copy-start(f32[256,2560]{0,1:T(8,128)} %get-tuple-element.73) | copy-start | bytes 7864324
  88.9 2.5 %copy-start.5 = (bf16[256,2560]{0,1:T(8,128)(2,1)S(1)}, bf16[256,2560]{0,1:T(8,128)(2,1)}, u32[]{:S(2)}) copy-start(bf16[256,2560]{0,1:T(8,128)(2,1)} %copy-done.4) | copy-start | bytes 3932164
  91.4 1.8 %copy-start.32 = (f32[256,2560]{0,1:T(8,128)S(1)}, f32[256,2560]{0,1:T(8,128)}, u32[]{:S(2)}) copy-start(f32[256,2560]{0,1:T(8,128)} %get-tuple-element.71) | copy-start | bytes 7864324
  93.3 1.7 %copy-start.3 = (bf16[256,2560]{0,1:T(8,128)(2,1)S(1)}, bf16[256,2560]{0,1:T(8,128)(2,1)}, u32[]{:S(2)}) copy-start(bf16[256,2560]{0,1:T(8,128)(2,1)} %copy-done.2) | copy-start | bytes 3932164
  95.0 0.9 copy-start.29
  95.0 1.8 %copy-start.31 = (f32[256,2560]{0,1:T(8,128)S(1)}, f32[256,2560]{0,1:T(8,128)}, u32[]{:S(2)}) copy-start(f32[256,2560]{0,1:T(8,128)} %get-tuple-element.69) | copy-start | bytes 7864324
  98.5 1.3 copy-start.8
  101.8 2.0 %copy-start.21 = (s32[2560]{0:T(1024)S(1)}, s32[2560]{0:T(1024)}, u32[]{:S(2)}) copy-start(s32[2560]{0:T(1024)} %copy-done.20) | copy-start | bytes 30724
  101.8 3.0 %copy-start.19 = (s32[2560]{0:T(1024)S(1)}, s32[2560]{0:T(1024)}, u32[]{:S(2)}) copy-start(s32[2560]{0:T(1024)} %copy-done.18) | copy-start | bytes 30724
  101.9 3.9 %copy-start.17 = (s32[2560]{0:T(1024)S(1)}, s32[2560]{0:T(1024)}, u32[]{:S(2)}) copy-start(s32[2560]{0:T(1024)} %copy-done.16) | copy-start | bytes 30724
  102.0 5.5 %copy-start.6 = (f32[256,256]{1,0:T(8,128)S(1)}, f32[256,256]{1,0:T(8,128)}, u32[]{:S(2)}) copy-start(f32[256,256]{1,0:T(8,128)} %fusion.52) | copy-start | bytes 786436
  102.0 5.5 %copy-start.15 = (f32[3,256]{1,0:T(4,128)S(1)}, f32[3,256]{1,0:T(4,128)}, u32[]{:S(2)}) copy-start(f32[3,256]{1,0:T(4,128)} %fusion.53) | copy-start | bytes 9220
  153.1 3.6 %copy-start.12 = (f32[2560]{0:T(1024)S(1)}, f32[2560]{0:T(1024)}, u32[]{:S(2)}) copy-start(f32[2560]{0:T(1024)} %get-tuple-element.54) | copy-start | bytes 30724
  153.1 3.6 %copy-start.11 = (f32[2560]{0:T(1024)S(1)}, f32[2560]{0:T(1024)}, u32[]{:S(2)}) copy-start(f32[2560]{0:T(1024)} %get-tuple-element.55) | copy-start | bytes 30724
  153.1 3.6 %copy-start.10 = (f32[2560]{0:T(1024)S(1)}, f32[2560]{0:T(1024)}, u32[]{:S(2)}) copy-start(f32[2560]{0:T(1024)} %get-tuple-element.56) | copy-start | bytes 30724
  (3 other events, 2.1 us)
Sparse Core Ops, SparseCore 0:
  36.2 47.9 reduce-scatter.1

commit v2 on v0

v2 whole, which is shorter than its diff:
```python
import functools
import math

import jax
import jax.numpy as jnp
from jax import lax
from jax.experimental import pallas as pl
from jax.experimental.pallas import tpu as pltpu
from jax.sharding import PartitionSpec as P

MESH = pl.DeviceIdType.MESH
ENTRY_COUNT, ATTRS, GAUSS = 20480, 59, 20480
HALF = GAUSS // 2
BLOCK, LANES = 128, 128
VIEWS, OWN = 8, 2560
CHAINS, SPREAD = 8, 4
WIDE, COLS, BONES, TABLE = 256, 512, 24, 192
PIECE, PLANE, DEPTH, HIGHS = 56, 16, 8, 4
ROWS = PIECE * PLANE


def scatter_kernel(rows_ref, ids_ref, grads_ref, out_ref, pos_ref, vals_a, vals_b, *accs):
    def zero(i, c):
        for a in accs:
            a[pl.ds(pl.multiple_of(i * 128, 128), 128), :] = jnp.zeros((128, 128), jnp.float32)
        return c

    lax.fori_loop(0, HALF // 128, zero, 0)

    def turn(off, vals):
        o = pl.multiple_of(off, 128)
        x = grads_ref[0, :, pl.ds(o, 128)].astype(jnp.float32)
        x = jnp.concatenate([x, jnp.zeros((64 - ATTRS, 128), jnp.float32)], axis=0)
        upper = ids_ref[:, pl.ds(o, 128)] >= HALF
        vals[...] = jnp.concatenate([jnp.where(upper, 0.0, x), jnp.where(upper, x, 0.0)], axis=0).T

    def add(off, vals):
        for j in range(BLOCK // CHAINS):
            r = [rows_ref[off + j * CHAINS + k] for k in range(CHAINS)]
            new = [
                accs[k][pl.ds(r[k], 1), :] + vals[j * CHAINS + k : j * CHAINS + k + 1, :]
                for k in range(CHAINS)
            ]
            for k in range(CHAINS):
                accs[k][pl.ds(r[k], 1), :] = new[k]

    turn(0, vals_a)

    def step(i, c):
        off = pl.multiple_of(i * (2 * BLOCK), 2 * BLOCK)
        turn(off + BLOCK, vals_b)
        add(off, vals_a)
        turn(jnp.minimum(off + 2 * BLOCK, ENTRY_COUNT - BLOCK), vals_a)
        add(off + BLOCK, vals_b)
        return c

    lax.fori_loop(0, ENTRY_COUNT // (2 * BLOCK), step, 0)

    def finish(i, c):
        for u in range(SPREAD):
            off = pl.multiple_of(i * (128 * SPREAD) + u * 128, 128)
            s = accs[0][pl.ds(off, 128), :]
            for a in accs[1:]:
                s = s + a[pl.ds(off, 128), :]
            t = s.T.astype(jnp.bfloat16)
            owner = off // OWN
            cols = pl.ds(pl.multiple_of(off - owner * OWN, 128), 128)
            out_ref[owner, :, cols] = t[:64]
            out_ref[owner + VIEWS // 2, :, cols] = t[64:]
            pos_ref[owner, :, cols] = t[:4]
            pos_ref[owner + VIEWS // 2, :, cols] = t[64:68]
        return c

    lax.fori_loop(0, HALF // (128 * SPREAD), finish, 0)


def scatter(grads, ids):
    vmem = pl.BlockSpec(memory_space=pltpu.VMEM)
    flat = ids.reshape(-1)
    return pl.pallas_call(
        scatter_kernel,
        out_shape=(
            jax.ShapeDtypeStruct((VIEWS, 64, OWN), jnp.bfloat16),
            jax.ShapeDtypeStruct((VIEWS, 4, OWN), jnp.bfloat16),
        ),
        in_specs=[pl.BlockSpec(memory_space=pltpu.SMEM), vmem, vmem],
        out_specs=(vmem, vmem),
        scratch_shapes=[pltpu.VMEM((BLOCK, 128), jnp.float32)] * 2
        + [pltpu.VMEM((HALF, 128), jnp.float32)] * CHAINS,
        compiler_params=pltpu.CompilerParams(vmem_limit_bytes=58 * 1024 * 1024),
        name="scatter",
    )(jnp.where(flat >= HALF, flat - HALF, flat), ids, grads)


def place():
    view, gauss = lax.axis_index("view"), lax.axis_index("gauss")
    return view // 2, lax.rem(view, 2), gauss // PLANE, lax.rem(gauss, PLANE)


def plane_peer(step):
    high, core, low, spot = place()
    return (high * 2 + core, low * PLANE + lax.rem(spot + step, PLANE))


def depth_peer(step):
    high, core, low, spot = place()
    level = lax.rem(high * 2 + low + step, DEPTH)
    return ((level // 2) * 2 + core, lax.rem(level, 2) * PLANE + spot)


def core_peer():
    high, core, low, spot = place()
    return (high * 2 + 1 - core, low * PLANE + spot)


def view_peer(step):
    return (lax.rem(lax.axis_index("view") + step, VIEWS), lax.axis_index("gauss"))


def high_peer(step):
    high, core, low, spot = place()
    return (lax.rem(high + step, HIGHS) * 2 + core, low * PLANE + spot)


def cross_peer(step):
    high, core, low, spot = place()
    return (lax.rem(high + step, HIGHS) * 2 + 1 - core, low * PLANE + spot)


def each(first, last, action):
    def one(step, carry):
        action(step)
        return carry

    lax.fori_loop(first, last, one, 0)


def greet(barrier, peer, count):
    each(
        1,
        count,
        lambda step: pl.semaphore_signal(
            barrier, inc=1, device_id=peer(step), device_id_type=MESH
        ),
    )


def remote(src, dst, sems, step, peer):
    return pltpu.make_async_remote_copy(
        src_ref=src,
        dst_ref=dst,
        send_sem=sems.at[0, step],
        recv_sem=sems.at[1, step],
        device_id=peer,
        device_id_type=MESH,
    )


def dot(left, right):
    return jnp.dot(left, right, preferred_element_type=jnp.float32)


def over_lanes(left, right):
    return lax.dot_general(
        left, right, (((1,), (1,)), ((), ())), preferred_element_type=jnp.float32
    )


def halves(value, count):
    parts = []
    for _ in range(count):
        part = value.astype(jnp.bfloat16)
        parts.append(part)
        value = value - part.astype(jnp.float32)
    return parts


def silu_pair(value):
    sig = 0.5 * jnp.tanh(0.5 * value) + 0.5
    act = value * sig
    return act.astype(jnp.bfloat16), sig + act * (1.0 - sig)


def step_kernel(
    factor,
    part,
    pos_part,
    feats,
    code_tab,
    subj,
    bone_ids,
    skin_w,
    canon,
    bone_tf,
    w_first,
    w_second,
    w_third,
    biases,
    w_head,
    attr_out,
    feat_out,
    skin_out,
    out,
    inputs,
    act_one,
    act_two,
    act_three,
    slope_one,
    slope_two,
    slope_three,
    back_one,
    back_two,
    back_three,
    hots,
    blends,
    points,
    shifts,
    turned,
    code_parts,
    bias_cols,
    head_rows,
    head_cols,
    bone_parts,
    bone_sum,
    bias_sum,
    subj_sum,
    pos_recv,
    half_recv,
    half_send,
    own_recv,
    pay,
    near,
    plane,
    depth,
    sems_pos,
    sems_half,
    sems_own,
    sems_near,
    sems_plane,
    sems_depth,
    sems_back,
):
    high, core, low, spot = place()
    view = high * 2 + core
    level = high * 2 + low
    barrier = pltpu.get_barrier_semaphore()
    greet(barrier, plane_peer, PLANE)
    greet(barrier, depth_peer, DEPTH)
    greet(barrier, cross_peer, HIGHS)
    pl.semaphore_signal(barrier, inc=1, device_id=core_peer(), device_id_type=MESH)
    pl.semaphore_wait(barrier, PLANE - 1 + DEPTH - 1 + HIGHS - 1 + 1)

    def pos_copy(step):
        return remote(
            pos_part.at[lax.rem(view + step, VIEWS)], pos_recv.at[view], sems_pos, step, view_peer(step)
        )

    def half_copy(step):
        slot = lax.rem(high + step, HIGHS)
        return remote(part.at[slot * 2 + 1 - core], half_recv.at[slot], sems_half, step, core_peer())

    def own_copy(step):
        return remote(
            half_send.at[lax.rem(high + step, HIGHS)], own_recv.at[high], sems_own, step, high_peer(step)
        )

    each(1, VIEWS, lambda step: pos_copy(step).start())
    half_order = lambda step: half_copy(step).start()
    each(1, HIGHS, half_order)
    half_order(0)
    pos_recv[view] = pos_part[view]

    turned[0] = w_first[...].T
    turned[1] = w_second[...].T
    turned[2] = w_third[...].T
    code_parts[...] = (
        jnp.concatenate([p.astype(jnp.float32) for p in halves(code_tab[...], 3)], axis=0)
        .T.astype(jnp.bfloat16)
    )
    bias_cols[...] = jnp.concatenate([biases[...], jnp.zeros((5, WIDE), jnp.float32)], axis=0).T
    head8 = jnp.concatenate(
        [w_head[...].astype(jnp.float32), jnp.zeros((5, WIDE), jnp.float32)], axis=0
    )
    head_rows[...] = head8.astype(jnp.bfloat16)
    head_cols[...] = head8.T.astype(jnp.bfloat16)
    blank = jnp.zeros((4, TABLE), jnp.float32)
    table = jnp.concatenate(
        [bone_tf[0:4], blank, bone_tf[4:8], blank, bone_tf[8:12], blank], axis=0
    )
    bone_parts[...] = jnp.concatenate(
        [p.astype(jnp.float32) for p in halves(table, 2)], axis=0
    ).astype(jnp.bfloat16)
    bone_sum[...] = jnp.zeros_like(bone_sum)
    bias_sum[...] = jnp.zeros_like(bias_sum)
    subj_sum[...] = jnp.zeros_like(subj_sum)

    def forward(chunk):
        cols = pl.ds(pl.multiple_of(chunk * COLS, COLS), COLS)
        subject = subj[:, cols]
        hot = (lax.rem(lax.broadcasted_iota(jnp.int32, (24, COLS), 0), 8) == subject).astype(
            jnp.float32
        ).astype(jnp.bfloat16)
        value = (feats[:, cols].astype(jnp.float32) + dot(code_parts[...], hot)).astype(jnp.bfloat16)
        inputs[:, cols] = value
        layers = (
            (w_first, act_one, slope_one),
            (w_second, act_two, slope_two),
            (w_third, act_three, slope_three),
        )
        for index, (weight, act, slope) in enumerate(layers):
            value, lean = silu_pair(dot(weight[...], value) + bias_cols[:, index : index + 1])
            act[:, cols] = value
            slope[:, cols] = lean
        rest = jnp.concatenate(
            [canon[0, :, cols], canon[1, :, cols], canon[2, :, cols], jnp.ones((1, COLS), jnp.float32),
             jnp.zeros((4, COLS), jnp.float32)],
            axis=0,
        )
        points[:, cols] = rest + dot(head_rows[...], value)
        index = lax.broadcasted_iota(jnp.int32, (TABLE, COLS), 0)
        for k in range(4):
            column = subject * BONES + bone_ids[k, :, cols]
            hot = (index == column).astype(jnp.float32).astype(jnp.bfloat16)
            hots[k, :, cols] = hot
            both = dot(bone_parts[...], hot)
            blends[k, :, cols] = both[:24] + both[24:]

    def own_start(step):
        half_copy(step).wait()
        slot = lax.rem(high + step, HIGHS)
        mine = part[slot * 2 + core].astype(jnp.float32)
        half_send[slot] = (mine + half_recv[slot].astype(jnp.float32)).astype(jnp.bfloat16)

    def own_send(step):
        own_start(step)
        own_copy(step).start()

    each(0, 2, forward)
    each(1, HIGHS, own_send)
    own_start(0)
    each(2, OWN // COLS, forward)
    each(1, VIEWS, lambda step: pos_copy(step).wait())

    def backward(chunk):
        cols = pl.ds(pl.multiple_of(chunk * COLS, COLS), COLS)
        pos = pos_recv[0, :, cols].astype(jnp.float32)
        for source in range(1, VIEWS):
            pos = pos + pos_recv[source, :, cols].astype(jnp.float32)
        pulls = [pos[i : i + 1] for i in range(3)]
        point = points[:, cols]
        shift = jnp.zeros((8, COLS), jnp.float32)
        for k in range(4):
            blend = blends[k, :, cols]
            moved = pulls[0] * blend[0:8] + pulls[1] * blend[8:16] + pulls[2] * blend[16:24]
            skin_out[k, :, cols] = jnp.sum(moved * point, axis=0, keepdims=True)
            weight = skin_w[k, :, cols]
            shift = shift + weight * moved
            spread = jnp.concatenate([(weight * pull) * point for pull in pulls], axis=0)
            pair = jnp.concatenate([p.astype(jnp.float32) for p in halves(spread, 2)], axis=0)
            bone_sum[...] += over_lanes(pair.astype(jnp.bfloat16), hots[k, :, cols])
        shift = shift.astype(jnp.bfloat16)
        shifts[:, cols] = shift
        value = (dot(head_cols[...], shift) * slope_three[:, cols]).astype(jnp.bfloat16)
        back_three[:, cols] = value
        tally(2, value)
        value = (dot(turned[2], value) * slope_two[:, cols]).astype(jnp.bfloat16)
        back_two[:, cols] = value
        tally(1, value)
        value = (dot(turned[1], value) * slope_one[:, cols]).astype(jnp.bfloat16)
        back_one[:, cols] = value
        hot = (lax.broadcasted_iota(jnp.int32, (8, COLS), 0) == subj[:, cols]).astype(
            jnp.float32
        ).astype(jnp.bfloat16)
        subj_sum[...] += over_lanes(hot, value)
        feat_out[:, cols] = dot(turned[0], value).astype(jnp.bfloat16)

    def tally(index, value):
        wide = value.astype(jnp.float32)
        total = bias_sum[index - 1]
        for lane in range(COLS // LANES):
            total = total + wide[:, lane * LANES : (lane + 1) * LANES]
        bias_sum[index - 1] = total

    each(0, OWN // COLS, backward)

    def store(row, value):
        count = value.shape[0]
        pay[0, row : row + count, :] = value[:, :LANES]
        pay[1, row : row + count, :] = value[:, LANES:]

    store(512, over_lanes(back_three[...], act_two[...]))
    store(256, over_lanes(back_two[...], act_one[...]))
    store(0, over_lanes(back_one[...], inputs[...]))
    store(768, over_lanes(shifts[...], act_three[...]))
    groups = subj_sum[...]
    store(
        776,
        jnp.concatenate(
            [jnp.sum(groups, axis=0, keepdims=True)]
            + [jnp.sum(bias_sum[index].T, axis=0, keepdims=True) for index in range(2)]
            + [jnp.zeros((5, WIDE), jnp.float32)],
            axis=0,
        ),
    )
    code = dot(
        jnp.concatenate([p.astype(jnp.float32) for p in halves(groups, 3)], axis=0).astype(jnp.bfloat16),
        w_first[...],
    )
    store(784, code[0:8] + code[8:16] + code[16:24])
    bone = bone_sum[0:24] + bone_sum[24:48]
    store(792, jnp.concatenate([bone, jnp.zeros((24, WIDE - TABLE), jnp.float32)], axis=1))
    store(816, jnp.zeros((ROWS - 816, WIDE), jnp.float32))

    def finish_attrs():
        each(1, HIGHS, lambda step: own_copy(step).wait())
        own_recv[high] = half_send[high]

        def piece(index):
            cols = pl.ds(pl.multiple_of(index * 256, 256), 256)
            total = own_recv[0, :, cols].astype(jnp.float32)
            for source in range(1, HIGHS):
                total = total + own_recv[source, :, cols].astype(jnp.float32)
            for row in range(ATTRS):
                attr_out[row, :, cols] = total[row : row + 1]

        each(0, OWN // 256, piece)

    reduce_all(
        factor, finish_attrs, pay, out, near, plane, depth, sems_near, sems_plane, sems_depth, sems_back
    )


def reduce_all(
    factor, cover, pay, out, near, plane, depth, sems_near, sems_plane, sems_depth, sems_back
):
    high, core, low, spot = place()
    level = high * 2 + low
    swap = remote(pay.at[1 - core], near, sems_near, 0, core_peer())
    swap.start()
    swap.wait()
    near[...] = near[...] + pay[core]

    def piece(index):
        return pl.ds(pl.multiple_of(index * PIECE, PIECE), PIECE)

    def plane_copy(step):
        return remote(
            near.at[piece(lax.rem(spot + step, PLANE))],
            plane.at[spot],
            sems_plane,
            step,
            plane_peer(step),
        )

    each(1, PLANE, lambda step: plane_copy(step).start())
    plane[spot] = near[piece(spot)]
    each(1, PLANE, lambda step: plane_copy(step).wait())
    total = plane[0]
    for index in range(1, PLANE):
        total = total + plane[index]
    depth[level] = total

    def depth_copy(step):
        return remote(depth.at[level], depth.at[level], sems_depth, step, depth_peer(step))

    each(1, DEPTH, lambda step: depth_copy(step).start())
    each(1, DEPTH, lambda step: depth_copy(step).wait())
    total = depth[0]
    for index in range(1, DEPTH):
        total = total + depth[index]
    out[core, piece(spot)] = total * factor

    def back_copy(step):
        return remote(
            out.at[core, piece(spot)], out.at[core, piece(spot)], sems_back, step, plane_peer(step)
        )

    each(1, PLANE, lambda step: back_copy(step).start())
    cover()
    each(1, PLANE, lambda step: back_copy(step).wait())
    last = remote(out.at[core], out.at[core], sems_near, 1, core_peer())
    last.start()
    last.wait()


def unpack_kernel(attrs, feats, skins, sums, attr_out, feat_out, skin_out, first, second, third, bias, head, code, bone):
    attr_out[...] = attrs[...]
    feat_out[...] = feats[...]
    skin_out[...] = skins[...]
    for half in range(2):
        lanes = slice(half * LANES, (half + 1) * LANES)
        first[:, lanes] = sums[half, 0:256]
        second[:, lanes] = sums[half, 256:512]
        third[:, lanes] = sums[half, 512:768]
        head[:, lanes] = sums[half, 768:771]
        bias[:, lanes] = sums[half, 776:779]
        code[:, lanes] = sums[half, 784:792]
        lanes = slice(half * LANES, min((half + 1) * LANES, TABLE))
        for i in range(3):
            start = 792 + 8 * i
            bone[4 * i : 4 * i + 4, lanes] = sums[half, start : start + 4, : lanes.stop - lanes.start]


def body(
    entry_grads,
    vis_ids,
    feats,
    code_tab,
    subj_ids,
    bone_ids,
    skin_w,
    canon_pos,
    bone_tf,
    w_first,
    w_second,
    w_third,
    biases,
    w_head,
):
    factor = 1.0 / math.sqrt(GAUSS * lax.axis_size("gauss"))
    part, pos_part = scatter(entry_grads, vis_ids)
    vmem = pl.BlockSpec(memory_space=pltpu.VMEM)
    f32, b16 = jnp.float32, jnp.bfloat16
    shape = jax.ShapeDtypeStruct
    sems = lambda count: pltpu.SemaphoreType.DMA((2, count))
    results = (
        shape((ATTRS, 1, OWN), f32),
        shape((WIDE, OWN), b16),
        shape((4, 1, OWN), f32),
    )
    values = pl.pallas_call(
        functools.partial(step_kernel, factor),
        out_shape=results + (shape((2, ROWS, LANES), f32),),
        in_specs=[vmem] * 14,
        out_specs=(vmem,) * 4,
        scratch_shapes=[pltpu.VMEM((WIDE, OWN), b16)] * 4
        + [pltpu.VMEM((WIDE, OWN), f32)] * 3
        + [pltpu.VMEM((WIDE, OWN), b16)] * 3
        + [
            pltpu.VMEM((4, TABLE, OWN), b16),
            pltpu.VMEM((4, 24, OWN), f32),
            pltpu.VMEM((8, OWN), f32),
            pltpu.VMEM((8, OWN), b16),
            pltpu.VMEM((3, WIDE, WIDE), b16),
            pltpu.VMEM((WIDE, 24), b16),
            pltpu.VMEM((WIDE, 8), f32),
            pltpu.VMEM((8, WIDE), b16),
            pltpu.VMEM((WIDE, 8), b16),
            pltpu.VMEM((48, TABLE), b16),
            pltpu.VMEM((48, TABLE), f32),
            pltpu.VMEM((2, WIDE, LANES), f32),
            pltpu.VMEM((8, WIDE), f32),
            pltpu.VMEM((VIEWS, 4, OWN), b16),
            pltpu.VMEM((HIGHS, 64, OWN), b16),
            pltpu.VMEM((HIGHS, 64, OWN), b16),
            pltpu.VMEM((HIGHS, 64, OWN), b16),
            pltpu.VMEM((2, ROWS, LANES), f32),
            pltpu.VMEM((ROWS, LANES), f32),
            pltpu.VMEM((PLANE, PIECE, LANES), f32),
            pltpu.VMEM((DEPTH, PIECE, LANES), f32),
            sems(VIEWS),
            sems(HIGHS),
            sems(HIGHS),
            sems(2),
            sems(PLANE),
            sems(DEPTH),
            sems(PLANE),
        ],
        compiler_params=pltpu.CompilerParams(
            collective_id=0, has_side_effects=True, vmem_limit_bytes=50 * 1024 * 1024
        ),
        name="step",
    )(
        part,
        pos_part,
        feats[:, 0],
        code_tab.T,
        subj_ids,
        bone_ids,
        skin_w,
        canon_pos,
        bone_tf,
        w_first,
        w_second,
        w_third,
        biases,
        w_head,
    )
    attrs, feat, skins, first, second, third, bias_rows, head, code, bone = pl.pallas_call(
        unpack_kernel,
        out_shape=results
        + (shape((WIDE, WIDE), f32),) * 3
        + (shape((3, WIDE), f32), shape((3, WIDE), f32), shape((8, WIDE), f32), shape((12, TABLE), f32)),
        in_specs=[vmem] * 4,
        out_specs=(vmem,) * 10,
        compiler_params=pltpu.CompilerParams(vmem_limit_bytes=16 * 1024 * 1024),
        name="unpack",
    )(*values)
    return (
        attrs,
        feat[:, None, :],
        skins,
        first,
        second,
        third,
        bias_rows,
        head,
        code.T,
        bone,
    )


def solution(mesh):
    placed = (
        P("view", None, "gauss"),
        P("view", "gauss"),
        P(None, "gauss", "view"),
        P(),
        P("gauss", "view"),
        P(None, "gauss", "view"),
        P(None, "gauss", "view"),
        P(None, "gauss", "view"),
        P(),
        P(),
        P(),
        P(),
        P(),
        P(),
    )
    return jax.shard_map(
        body,
        mesh=mesh,
        in_specs=placed,
        out_specs=(
            P(None, "gauss", "view"),
            P(None, "gauss", "view"),
            P(None, "gauss", "view"),
            P(),
            P(),
            P(),
            P(),
            P(),
            P(),
            P(),
        ),
        check_vma=False,
    )
```

time: 491 us -> 95.3 us (0.19)
  waiting for transfers between devices: 206 us -> 0 us
  other arithmetic: 124 us -> 1.53 us
  Pallas kernels: 0 us -> 91.7 us
  blocking collectives: 81 us -> 0 us
  local copies, waits for them, and re-layouts: 32.5 us -> 0.97 us
  matrix products: 31.1 us -> 0 us
  between operations: 14.5 us -> 0.79 us
    psum x1 -> x0, waiting for transfers between devices: 174 us -> none  [body(): lax.psum((first, second, third, bias_one, bias_two, bias_three, head, cod...]
    scatter-add x1 -> x0, other arithmetic: 114 us -> none  [body(): partial_value = jnp.zeros((entry_grads.shape[1], member_count * viewers),...]
    pallas_call x0 -> x3, Pallas kernels: none -> 91.7 us  [the longest x1 62.4 us: body(): pl.pallas_call(functools.partial(step_kernel, factor), out_shape=results...]
    psum x1 -> x0, blocking collectives: 81 us -> none  [body(): lax.psum((first, second, third, bias_one, bias_two, bias_three, head, cod...]
    reduce_scatter x1 -> x0, waiting for transfers between devices: 31.7 us -> none  [body(): lax.psum_scatter(partial_value.astype(jnp.bfloat16), 'view', scatter_dime...]
    dot_general x22 -> x0, matrix products: 31.1 us -> none  [the longest x4 6.74 us: body(): lax.dot_general(contribution, onehot, (((1,), (1,)), ((), ())), precision...]
    unnamed x80 -> x24, local copies, waits for them, and re-layouts: 13.5 us -> 0.97 us
    convert_element_type x1 -> x0, local copies, waits for them, and re-layouts: 8.61 us -> none  [body(): entry_grads[0].astype(jnp.float32)]
  transfers between devices with their start and end apart: 2 -> 0, of which waited for: 2 -> 0; matrix products, arithmetic and copies ran while one was open for 3% -> 0% of each run, Pallas kernels for 0% -> 0%
where the time goes in v2:
time: 95.3 us; the launch traced here: 95 us
  Pallas kernels  91.7 us (96%)
  other arithmetic  1.53 us (2%)
  local copies, waits for them, and re-layouts  0.97 us (1%)
    pallas_call x1, Pallas kernels, body(): pl.pallas_call(functools.partial(step_kernel, factor), out_shape=results...  62.4 us
    pallas_call x1, Pallas kernels, scatter(): pl.pallas_call(scatter_kernel, out_shape=(jax.ShapeDtypeStruct((VIEWS, 64...  27.5 us

profile of v2, /device:TPU:1, one launch (start us, length us, event | category | flops | bytes accessed | tf_op | source)
XLA Modules:
  0.0 95.0 jit_solution(8076103117131102338)
XLA Ops:
  0.6 1.5 %compare_select_fusion.rows_ref = s32[20480]{0:T(1024)} fusion(s32[20480]{0:T(1024)} %bitcast.7), kind=kLoop, calls=%fused_computation | loop fusion | flops 61440 | bytes 163840 | tf_op jit(solution)/shard_map/jit(_where)/select_n | solution.py:92
  2.2 0.0 copy-start.1
  2.2 0.0 copy-start.2
  2.2 0.0 copy-start.3
  2.2 0.0 copy-start.4
  2.2 0.0 copy-start.5
  2.2 0.0 copy-start.6
  2.2 0.0 copy-start.7
  2.2 0.0 copy-start.8
  2.2 0.0 copy-start.9
  2.2 0.0 copy-start.10
  2.3 0.0 copy-start.11
  2.3 27.5 %scatter.1 = (bf16[8,64,2560]{2,1,0:T(8,128)(2,1)}, bf16[8,4,2560]{2,1,0:T(4,128)(2,1)}) custom-call(s32[20480]{0:T(1024)} %compare_select_fusion.rows_ref, s32[1,20480]{1,0:T(1,128)} %ids_ref.1, bf16[1,59,20480]{2,1,0:T(8,128)(2,1)} %grads_ref.1), custom_call_target="tpu_custom_call" | custom-call | tf_op jit(solution)/shard_map/scatter/pallas_call | solution.py:80
  29.8 0.0 copy-done.1
  29.8 0.0 copy-done.2
  29.8 0.0 copy-done.3
  29.8 0.0 copy-done.4
  29.8 0.0 copy-done.5
  29.8 0.0 copy-done.6
  29.8 0.0 copy-done.7
  29.8 0.0 copy-done.8
  29.9 0.0 copy-done.9
  29.9 0.0 copy-done.10
  29.9 0.0 copy-done.11
  29.9 0.0 copy-start
  29.9 0.9 copy-done
  30.8 62.4 %step.1 = (f32[59,1,2560]{2,1,0:T(1,128)S(1)}, bf16[256,2560]{1,0:T(8,128)(2,1)S(1)}, f32[4,1,2560]{2,1,0:T(1,128)S(1)}, f32[2,896,128]{2,1,0:T(8,128)S(1)}) custom-call(bf16[8,64,2560]{2,1,0:T(8,128)(2,1)} %get-tuple-element.26.part, bf16[8,4,2560]{2,1,0:T(4,128)(2,1)S(1)} %copy-done, bf16[256,2560]{1,0:T(8,128)(2,1)} %bitcast.6, f32[8,256]{1,0:T(8,128)S(1)} %bitcast.5, ...), custom_call_target="tpu_custom_call" | custom-call | tf_op jit(solution)/shard_map/step/pallas_call | solution.py:531
  93.2 1.7 %unpack.1 = (f32[59,1,2560]{2,1,0:T(1,128)}, bf16[256,2560]{1,0:T(8,128)(2,1)}, f32[4,1,2560]{2,1,0:T(1,128)}, f32[256,256]{1,0:T(8,128)}, f32[256,256]{1,0:T(8,...) custom-call(f32[59,1,2560]{2,1,0:T(1,128)S(1)} %get-tuple-element.28, ...), custom_call_target="tpu_custom_call" | custom-call | tf_op jit(solution)/shard_map/unpack/pallas_call | solution.py:589
Async XLA Ops:
  2.2 27.6 %copy-start.1 = (bf16[256,256]{1,0:T(8,128)(2,1)S(1)}, bf16[256,256]{1,0:T(8,128)(2,1)}, u32[]{:S(2)}) copy-start(bf16[256,256]{1,0:T(8,128)(2,1)} %w_first.1) | copy-start | bytes 393220
  2.2 27.6 %copy-start.2 = (bf16[256,256]{1,0:T(8,128)(2,1)S(1)}, bf16[256,256]{1,0:T(8,128)(2,1)}, u32[]{:S(2)}) copy-start(bf16[256,256]{1,0:T(8,128)(2,1)} %w_second.1) | copy-start | bytes 393220
  2.2 27.6 %copy-start.3 = (bf16[256,256]{1,0:T(8,128)(2,1)S(1)}, bf16[256,256]{1,0:T(8,128)(2,1)}, u32[]{:S(2)}) copy-start(bf16[256,256]{1,0:T(8,128)(2,1)} %w_third.1) | copy-start | bytes 393220
  2.2 27.6 %copy-start.4 = (s32[4,1,2560]{2,1,0:T(1,128)S(1)}, s32[4,1,2560]{2,1,0:T(1,128)}, u32[]{:S(2)}) copy-start(s32[4,1,2560]{2,1,0:T(1,128)} %bone_ids.1) | copy-start | bytes 122884
  2.2 27.6 %copy-start.5 = (f32[4,1,2560]{2,1,0:T(1,128)S(1)}, f32[4,1,2560]{2,1,0:T(1,128)}, u32[]{:S(2)}) copy-start(f32[4,1,2560]{2,1,0:T(1,128)} %skin_w.1) | copy-start | bytes 122884
  2.2 27.6 %copy-start.6 = (f32[3,1,2560]{2,1,0:T(1,128)S(1)}, f32[3,1,2560]{2,1,0:T(1,128)}, u32[]{:S(2)}) copy-start(f32[3,1,2560]{2,1,0:T(1,128)} %canon.1) | copy-start | bytes 92164
  2.2 27.6 %copy-start.7 = (f32[12,192]{1,0:T(8,128)S(1)}, f32[12,192]{1,0:T(8,128)}, u32[]{:S(2)}) copy-start(f32[12,192]{1,0:T(8,128)} %bone_tf.1) | copy-start | bytes 27652
  2.2 27.6 %copy-start.8 = (s32[1,2560]{1,0:T(1,128)S(1)}, s32[1,2560]{1,0:T(1,128)}, u32[]{:S(2)}) copy-start(s32[1,2560]{1,0:T(1,128)} %subj.1) | copy-start | bytes 30724
  2.2 27.6 %copy-start.9 = (f32[256,8]{0,1:T(8,128)S(1)}, f32[256,8]{0,1:T(8,128)}, u32[]{:S(2)}) copy-start(f32[256,8]{0,1:T(8,128)} %param.17) | copy-start | bytes 24580
  2.2 27.6 %copy-start.10 = (f32[3,256]{1,0:T(4,128)S(1)}, f32[3,256]{1,0:T(4,128)}, u32[]{:S(2)}) copy-start(f32[3,256]{1,0:T(4,128)} %biases.1) | copy-start | bytes 9220
  2.3 27.6 %copy-start.11 = (bf16[3,256]{1,0:T(4,128)(2,1)S(1)}, bf16[3,256]{1,0:T(4,128)(2,1)}, u32[]{:S(2)}) copy-start(bf16[3,256]{1,0:T(4,128)(2,1)} %w_head.1) | copy-start | bytes 4612
  29.9 0.9 copy-start
